TPU v7x, 256 devices: a whole 4x4x8 slice. The times are simulated.
256 devices in a mesh: ctx: 32 (over x, y, core), head: 8 (over z).
Axes of the slice: x: 4, y: 4, z: 8, core: 2. Of those that a mesh axis runs over, the one named last changes fastest.
Arguments:
- lin_q: bfloat16 [8192, 8192], P('ctx', 'head'), may hold values from -4 to 4
- lin_k: bfloat16 [8192, 8192], P('ctx', 'head'), may hold values from -4 to 4
- lin_v: bfloat16 [8192, 8192], P('ctx', 'head'), may hold values from -6 to 6
- log_decay: float32 [64, 8192], P('head', 'ctx'), may hold values from -1 to 0
- lin_gain: float32 [8192], P('head'), may hold values from 0.1 to 1.9
- soft_q: bfloat16 [8192, 8192], P(('ctx', 'head')), may hold values from -200 to 200
- soft_kv: bfloat16 [8192, 2048], P(('ctx', 'head')), may hold values from -8 to 8
Outputs:
- lin_out: bfloat16 [8192, 8192], P('ctx', 'head')
- soft_out: bfloat16 [8192, 8192], P(('ctx', 'head'))
All inputs are finite; a program needn't handle non-finite values.
Results may differ from a plain program's by a relative error of at most 0.013.
Values may be sent and summed in bfloat16 or wider, within the bound.
No kernel may reach another device: no remote copies, remote signals or barrier semaphores. Data moves between devices by JAX's collectives and lax.ppermute only.
A program may use at most 64 MiB of HBM per device.

v0:
```python
import math
import jax
import jax.numpy as jnp
from jax import lax
from jax.sharding import Mesh
from jax.sharding import PartitionSpec as P

CTX = ("ctx_0", "ctx_1", "ctx_2")
CTX_HEAD = ("ctx_0", "ctx_1", "ctx_2", "head")


def filled_with(value, identity):
    return jax.tree.map(
        lambda part, zero: jnp.zeros_like(part) + jnp.asarray(zero, part.dtype), value, identity
    )


def carried_in(value, axes, combine, identity):
    before = start = filled_with(value, identity)
    so_far = value
    for axis in reversed(axes):
        devices, index = (lax.axis_size(axis), lax.axis_index(axis))
        pieces = jax.tree.map(
            lambda part, kind: lax.all_gather(part.astype(kind), axis),
            so_far,
            (jnp.bfloat16, jnp.bfloat16),
        )
        inside, so_far = (start, start)
        for k in range(devices):
            passed = k < index
            so_far = combine(
                so_far, jax.tree.map(lambda part, own: part[k].astype(own.dtype), pieces, value)
            )
            inside = jax.tree.map(lambda new, old: jnp.where(passed, new, old), so_far, inside)
        before = combine(inside, before)
    return before


def block_local(kb, gb):
    cum = jnp.cumsum(gb, axis=1)
    keys_scaled = (kb.astype(jnp.float32) * jnp.exp(cum[:, -1:] - cum).T[:, :, None]).astype(
        jnp.bfloat16
    )
    return (cum, keys_scaled)


def block_output(qb, kb, vb, cum, state):
    size = cum.shape[1]
    pos = jnp.arange(size)
    causal = pos[:, None] >= pos[None, :]
    diff = cum[:, :, None] - cum[:, None, :]
    weight = jnp.where(causal[None], jnp.exp(jnp.minimum(diff, 0.0)), 0.0)
    scores = jnp.einsum("thd,shd->hts", qb, kb, preferred_element_type=jnp.float32)
    probs = (scores * weight).astype(jnp.bfloat16)
    intra = jnp.einsum("hts,shd->thd", probs, vb, preferred_element_type=jnp.float32)
    inter = jnp.einsum(
        "thd,hde->the", qb, state.astype(jnp.bfloat16), preferred_element_type=jnp.float32
    )
    return intra + jnp.exp(cum).T[:, :, None] * inter


def join_states(earlier, later):
    return (earlier[0] + later[0], jnp.exp(later[0])[:, None, None] * earlier[1] + later[1])


def lightning_part(lin_q, lin_k, lin_v, log_decay, lin_gain):
    tok, width = lin_q.shape
    heads = log_decay.shape[0]
    dim = width // heads
    q = lin_q.reshape(tok, heads, dim)
    k = lin_k.reshape(tok, heads, dim)
    v = lin_v.reshape(tok, heads, dim)
    total = (jnp.zeros((heads,), jnp.float32), jnp.zeros((heads, dim, dim), jnp.float32))
    cum, keys_scaled = block_local(k, log_decay)
    local = jnp.einsum("shd,she->hde", keys_scaled, v, preferred_element_type=jnp.float32)
    total = join_states(total, (cum[:, -1], local))
    identity = (jnp.zeros((heads,), jnp.float32), jnp.zeros((heads, dim, dim), jnp.float32))
    entering = carried_in((total[0], total[1]), CTX, join_states, identity)
    state = entering[1]
    mixed = block_output(q, k, v, cum, state)
    rms = jnp.sqrt(jnp.mean(mixed * mixed, axis=-1, keepdims=True) + 1e-05)
    outputs = mixed / rms * lin_gain.reshape(heads, dim)
    return outputs.reshape(tok, width).astype(jnp.bfloat16)


def softmax_part(soft_q, soft_kv, dim):
    local_q, local_kv = (
        lax.all_to_all(soft_q, "head", split_axis=1, concat_axis=0, tiled=True),
        lax.all_to_all(soft_kv, "head", split_axis=1, concat_axis=0, tiled=True),
    )
    tok = local_q.shape[0]
    half = tok // 2
    kvl = local_kv.shape[1] // (2 * dim)
    group = local_q.shape[1] // (dim * kvl)
    mine = lax.axis_index(CTX)
    first_q = local_q[:half]
    second_q = local_q[half:]
    second_start = mine * tok + half
    first_start = mine * tok
    first_pos = first_start + jnp.arange(half)
    second_pos = second_start + jnp.arange(half)
    first_heads = first_q.reshape(half, kvl, group, dim)
    second_heads = second_q.reshape(half, kvl, group, dim)
    scale = dim ** (-0.5)

    def update(carry, queries, qpos, kblock, kstart):
        peak, total, acc = carry
        size = kblock.shape[0]
        pair = kblock.reshape(size, kvl, 2, dim)
        key_matrix = pair[:, :, 0]
        value_rows = pair[:, :, 1]
        kpos = kstart + jnp.arange(size)
        mask = (kpos[None, :] <= qpos[:, None])[None, None]
        scores = (
            jnp.einsum("qngd,knd->ngqk", queries, key_matrix, preferred_element_type=jnp.float32)
            * scale
        )
        scores = jnp.where(mask, scores, -1e30)
        newpeak = jnp.maximum(peak, jnp.max(scores, axis=-1))
        weights = jnp.where(mask, jnp.exp(scores - newpeak[..., None]), 0.0)
        decay_factor = jnp.exp(peak - newpeak)
        total = total * decay_factor + jnp.sum(weights, axis=-1)
        acc = acc * decay_factor[..., None] + jnp.einsum(
            "ngqk,knd->ngqd",
            weights.astype(jnp.bfloat16),
            value_rows,
            preferred_element_type=jnp.float32,
        )
        return (newpeak, total, acc)

    def guarded(carry, queries, qpos, qlast, kblock, kstart):
        return lax.cond(
            kstart <= qlast, lambda c: update(c, queries, qpos, kblock, kstart), lambda c: c, carry
        )

    def start_carry():
        return (
            jnp.full((kvl, group, half), -1e30, jnp.float32),
            jnp.zeros((kvl, group, half), jnp.float32),
            jnp.zeros((kvl, group, half, dim), jnp.float32),
        )

    def finish(carry):
        peak, total, acc = carry
        result = acc / total[..., None]
        return result.transpose(2, 0, 1, 3).reshape(half, kvl * group * dim).astype(jnp.bfloat16)

    piece = lax.all_gather(local_kv, CTX, axis=0, tiled=True)
    rows = piece.shape[0]
    width = math.gcd(rows, 512)

    def step(index, inner):
        kblock = lax.dynamic_slice_in_dim(piece, index * width, width, 0)
        kstart = index * width
        early = guarded(inner[0], first_heads, first_pos, first_start + half - 1, kblock, kstart)
        later = guarded(inner[1], second_heads, second_pos, second_start + half - 1, kblock, kstart)
        return (early, later)

    early, later = lax.fori_loop(0, rows // width, step, (start_carry(), start_carry()))
    first_out = finish(early)
    second_out = finish(later)
    result = jnp.concatenate([first_out, second_out], axis=0)
    return lax.all_to_all(result, "head", split_axis=0, concat_axis=1, tiled=True)


def body(lin_q, lin_k, lin_v, log_decay, lin_gain, soft_q, soft_kv):
    heads = log_decay.shape[0]
    dim = lin_q.shape[1] // heads
    lin_out = lightning_part(lin_q, lin_k, lin_v, log_decay, lin_gain)
    soft_out = softmax_part(soft_q, soft_kv, dim)
    return (lin_out, soft_out)


def solution(mesh):
    finer = Mesh(
        mesh.devices.reshape(4, 4, 2, mesh.shape["head"]), ("ctx_0", "ctx_1", "ctx_2", "head")
    )
    placed = (
        P(CTX, "head"),
        P(CTX, "head"),
        P(CTX, "head"),
        P("head", CTX),
        P("head"),
        P(CTX_HEAD, None),
        P(CTX_HEAD, None),
    )
    return jax.shard_map(
        body,
        mesh=finer,
        in_specs=placed,
        out_specs=(P(CTX, "head"), P(CTX_HEAD, None)),
        check_vma=False,
    )
```

profile of v0, /device:TPU:31, one launch (start us, length us, event | category | flops | bytes accessed | tf_op | source)
XLA Modules:
  0.0 221.1 jit_solution(15442327545542827741)
XLA Ops:
  7.2 1.3 reduce-window.6
  11.4 2.8 %all-reduce = bf16[16]{0:T(256)(128)(2,1)S(1)} all-reduce(bf16[16]{0:T(256)(128)(2,1)S(1)} %dynamic-update-slice), channel_id=2, replica_groups=mesh['ctx_0'=4,'ctx_1'=4,'ctx_2'=2,'head'=8] {'ctx_2'}, use_global_device_ids=true, to_apply=%add | all-reduce | flops 16 | bytes 64
  16.4 1.3 fusion.42
  17.7 2.2 all-gather.1
  20.9 16.0 %all_to_all.54 = bf16[32,8,256]{2,0,1:T(8,128)(2,1)} all-to-all(bf16[32,8,256]{2,0,1:T(8,128)(2,1)S(1)} %bitcast.354), channel_id=1, replica_groups=mesh['ctx_0'=4,'ctx_1'=4,'ctx_2'=2,'head'=8] {'head'}, dimensions={1} | all-to-all | bytes 262144 | tf_op jit(solution)/shard_map/all_to_all | solution.py:89
  37.8 3.5 %all-to-all-start.1 = ((bf16[32,8,1024]{2,0,1:T(8,128)(2,1)}), bf16[32,8,1024]{2,0,1:T(8,128)(2,1)S(1)}, u32[]{:S(2)}, u32[]{:S(2)}) async-start(bf16[32,8,1024]{2,0,1:T(8,128)(2,1)} %bitcast.330), calls=%async_computation.1 | async-start | bytes 1048576 | tf_op jit(solution)/shard_map/all_to_all | solution.py:88
  41.4 5.2 %all-gather.2 = bf16[4,1,8]{2,1,0:T(2,128)(2,1)S(1)} all-gather(bf16[1,1,8]{2,1,0:T(2,128)(2,1)S(1)} %get-tuple-element.626), channel_id=1, replica_groups=mesh['ctx_0'=4,'ctx_1'=4,'ctx_2'=2,'head'=8] {'ctx_1'}, dimensions={0}, use_global_device_ids=true | all-gather | bytes 80 | tf_op jit(solution)/shard_map/all_gather | solution.py:24
  46.6 5.3 %all-gather.3 = bf16[4,1,8]{2,1,0:T(2,128)(2,1)S(1)} all-gather(bf16[1,1,8]{2,1,0:T(2,128)(2,1)S(1)} %get-tuple-element.620), channel_id=1, replica_groups=mesh['ctx_0'=4,'ctx_1'=4,'ctx_2'=2,'head'=8] {'ctx_0'}, dimensions={0}, use_global_device_ids=true | all-gather | bytes 80 | tf_op jit(solution)/shard_map/all_gather | solution.py:24
  52.0 5.0 %all-to-all-done.1 = bf16[32,8,1024]{2,0,1:T(8,128)(2,1)S(1)} async-done(((bf16[32,8,1024]{2,0,1:T(8,128)(2,1)}), bf16[32,8,1024]{2,0,1:T(8,128)(2,1)S(1)}, u32[]{:S(2)}, u32[]{:S(2)}) %all-to-all-start.1) | async-done | bytes 524320 | tf_op jit(solution)/shard_map/all_to_all | solution.py:88
  57.3 2.3 %fusion.66 = bf16[1,8,128,128]{3,2,1,0:T(8,128)(2,1)} fusion(f32[8]{0:T(128)S(1)} %get-tuple-element.624, f32[8]{0:T(128)S(1)} %get-tuple-element.623, f32[8]{0:T(128)S(1)} %get-tuple-element.622, f32[8]{0:T(128)S(1)} %get-tuple-element.621, bf16[4,8,128,128]{3,2,1,0:T(8,128)(2,1)} %all-gather.8.cloned.1.call-done), kind=kLoop, calls=%fused_computation.103 | loop fusion | flops 1572864 | bytes 1310848 | tf_op jit(solution)/shard_map/convert_element_type | solution.py:24
  59.6 42.5 %all-gather.12.cloned.1.call-done = bf16[8192,256]{1,0:T(8,128)(2,1)} async-done(((bf16[256,256]{1,0:T(8,128)(2,1)}), bf16[8192,256]{1,0:T(8,128)(2,1)}) %all-gather.12.cloned.1.call-update) | async-done | bytes 4194320 | tf_op jit(solution)/shard_map/all_gather | solution.py:148
  102.3 85.3 %while.27 = (s32[]{:T(128)}, f32[1,8,128]{2,1,0:T(8,128)S(1)}, f32[1,8,128]{2,1,0:T(8,128)S(1)}, f32[1,8,128,128]{3,2,1,0:T(8,128)S(1)}, f32[1,8,128]{2,1,0:T(8,...) while((s32[]{:T(128)}, f32[1,8,128]{2,1,0:T(8,128)S(1)}, ...), condition=%wide.region_12.13_spmd.clone, body=%wide.region_3.12_spmd.clone.sunk | while | flops 551165184 | bytes 17445364 | solution.py:159
  103.4 2.1 conditional.7
  105.5 2.1 conditional.6
  108.8 2.1 conditional.7
  110.8 2.1 conditional.6
  114.1 2.1 conditional.7
  116.2 2.1 conditional.6
  119.4 2.1 conditional.7
  121.5 2.1 conditional.6
  124.7 2.1 conditional.7
  126.8 2.1 conditional.6
  130.1 2.1 conditional.7
  132.2 2.1 conditional.6
  135.4 2.1 conditional.7
  137.5 2.1 conditional.6
  140.7 2.1 conditional.7
  142.8 2.1 conditional.6
  146.1 2.1 conditional.7
  148.1 2.1 conditional.6
  151.4 2.1 conditional.7
  153.5 2.1 conditional.6
  156.7 2.1 conditional.7
  158.8 2.1 conditional.6
  162.0 2.1 conditional.7
  164.1 2.1 conditional.6
  167.4 2.1 conditional.7
  169.5 2.1 conditional.6
  172.7 2.1 conditional.7
  174.8 2.1 conditional.6
  178.0 2.1 conditional.7
  180.1 2.1 conditional.6
  183.4 2.1 conditional.7
  185.5 2.1 conditional.6
  189.2 6.7 %all-to-all-start.2 = ((bf16[8,32,1024]{2,1,0:T(8,128)(2,1)}), bf16[8,32,1024]{2,1,0:T(8,128)(2,1)S(1)}, u32[]{:S(2)}, u32[]{:S(2)}) async-start(bf16[8,32,1024]{2,1,0:T(8,128)(2,1)} %bitcast.73), calls=%async_computation.2 | async-start | bytes 1048576 | tf_op jit(solution)/shard_map/all_to_all | solution.py:163
  195.9 3.6 %fusion.41 = f32[256,8,128]{0,2,1:T(8,128)} fusion(f32[256,8]{0,1:T(8,128)S(1)} %get-tuple-element.608, bf16[4,8,128,128]{3,2,1,0:T(8,128)(2,1)} %all-gather.10.cloned.1.call-done, f32[8]{0:T(128)S(1)} %get-tuple-element.627, f32[8]{0:T(128)S(1)} %get-tuple-element.625, f32[8]{0:T(128)S(1)} %get-tuple-element.624, f32[8]{0:T(128)S(1)} %get-tuple-element.623, ...), kind=kOutput, calls=%fused_computation.62 | convolution fusion | flops 72876032 | bytes 4202890 | tf_op jit(solution)/shard_map/thd,hde->the/dot_general | solution.py:56
  199.5 2.4 %multiply_reduce_fusion = (f32[256,8]{0,1:T(8,128)S(1)}, f32[256,8,128]{0,2,1:T(8,128)S(1)}) fusion(f32[256,8,128]{0,2,1:T(8,128)} %fusion.41, bf16[256,8,128]{0,2,1:T(8,128)(2,1)S(1)} %bitcast.351, f32[8,256]{1,0:T(8,128)S(1)} %get-tuple-element.609, pred[256,256]{1,0:T(8,128)(4,1)S(1)} %iota_compare_fusion, bf16[256,1024]{1,0:T(8,128)(2,1)} %param.15, ...), kind=kOutput, calls=%fused_computation.66 | convolution fusion | flops 271841280 | bytes 3751936 | tf_op jit(solution)/shard_map/hts,shd->thd/dot_general | solution.py:55
  203.1 10.7 %all-to-all-done.2 = bf16[8,32,1024]{2,1,0:T(8,128)(2,1)S(1)} async-done(((bf16[8,32,1024]{2,1,0:T(8,128)(2,1)}), bf16[8,32,1024]{2,1,0:T(8,128)(2,1)S(1)}, u32[]{:S(2)}, u32[]{:S(2)}) %all-to-all-start.2) | async-done | bytes 524320 | tf_op jit(solution)/shard_map/all_to_all | solution.py:163
  (414 shorter events, 91.9 us)
Async XLA Ops:
  7.2 188.7 %copy-start = (bf16[256,1024]{1,0:T(8,128)(2,1)S(1)}, bf16[256,1024]{1,0:T(8,128)(2,1)}, u32[]{:S(2)}) copy-start(bf16[256,1024]{1,0:T(8,128)(2,1)} %param.13) | copy-start | bytes 1572868
  7.2 50.1 %all-gather.8.cloned.1.call-start = ((), (), s32[]{:S(2)}) async-start(), calls=%async_computation.3 | async-start | bytes 1310720 | tf_op jit(solution)/shard_map/all_gather | solution.py:24
  14.3 6.6 %copy-start.4 = (bf16[32,2048]{1,0:T(8,128)(2,1)S(1)}, bf16[32,2048]{1,0:T(8,128)(2,1)}, u32[]{:S(2)}) copy-start(bf16[32,2048]{1,0:T(8,128)(2,1)} %param.19) | copy-start | bytes 393220
  15.6 0.8 copy-start.2
  15.6 21.4 %copy-start.1 = (bf16[32,8192]{1,0:T(8,128)(2,1)S(1)}, bf16[32,8192]{1,0:T(8,128)(2,1)}, u32[]{:S(2)}) copy-start(bf16[32,8192]{1,0:T(8,128)(2,1)} %param.18) | copy-start | bytes 1572868
  20.8 81.3 %all-gather.12.cloned.1.call-start = ((), (), s32[]{:S(2)}) async-start(), calls=%async_computation.5 | async-start | bytes 4325376 | tf_op jit(solution)/shard_map/all_gather | solution.py:148
  37.8 19.2 %all-to-all-start.1 = ((bf16[32,8,1024]{2,0,1:T(8,128)(2,1)}), bf16[32,8,1024]{2,0,1:T(8,128)(2,1)S(1)}, u32[]{:S(2)}, u32[]{:S(2)}) async-start(bf16[32,8,1024]{2,0,1:T(8,128)(2,1)} %bitcast.330), calls=%async_computation.1 | async-start | bytes 1048576 | tf_op jit(solution)/shard_map/all_to_all | solution.py:88
  41.3 154.5 %all-gather.10.cloned.1.call-start = ((), (), s32[]{:S(2)}) async-start(), calls=%async_computation.4 | async-start | bytes 1310720 | tf_op jit(solution)/shard_map/all_gather | solution.py:24
  189.2 24.6 %all-to-all-start.2 = ((bf16[8,32,1024]{2,1,0:T(8,128)(2,1)}), bf16[8,32,1024]{2,1,0:T(8,128)(2,1)S(1)}, u32[]{:S(2)}, u32[]{:S(2)}) async-start(bf16[8,32,1024]{2,1,0:T(8,128)(2,1)} %bitcast.73), calls=%async_computation.2 | async-start | bytes 1048576 | tf_op jit(solution)/shard_map/all_to_all | solution.py:163
  195.9 3.6 %copy-start.3 = (bf16[256,1024]{0,1:T(8,128)(2,1)S(1)}, bf16[256,1024]{0,1:T(8,128)(2,1)}, u32[]{:S(2)}) copy-start(bf16[256,1024]{0,1:T(8,128)(2,1)} %copy-done.2) | copy-start | bytes 1572868
  199.5 2.4 %copy-start.5 = (f32[1024]{0:T(1024)S(1)}, f32[1024]{0:T(1024)}, u32[]{:S(2)}) copy-start(f32[1024]{0:T(1024)} %param.17) | copy-start | bytes 12292
Sparse Core Ops, SparseCore 0:
  20.9 26.1 all-gather.7
  49.7 52.4 all-gather.11
  104.5 25.1 all-gather.9
where the time goes:
time: 222 us; the launch traced here: 221 us
  waiting for transfers between devices  58.3 us (26%)
  matrix products  49.3 us (22%)
  blocking collectives  31.5 us (14%)
  other arithmetic  26.8 us (12%)
  local copies, waits for them, and re-layouts  26.5 us (12%)
  between operations  14.7 us (7%)
  starting transfers between devices  10.3 us (5%)
  loops' own time  3.78 us (2%)
    all_gather x1, waiting for transfers between devices, softmax_part(): piece = lax.all_gather(local_kv, CTX, axis=0, tiled=True)  42.5 us
    dot_general x32, matrix products, update(): jnp.einsum('ngqk,knd->ngqd', weights.astype(jnp.bfloat16), value_rows, pr...  26.6 us
    dynamic_slice x32, local copies, waits for them, and re-layouts, step(): kblock = lax.dynamic_slice_in_dim(piece, index * width, width, 0)  17.8 us
    reduce_sum x32, other arithmetic, update(): total = total * decay_factor + jnp.sum(weights, axis=-1)  16.4 us
    all_to_all x1, blocking collectives, softmax_part(): lax.all_to_all(soft_kv, 'head', split_axis=1, concat_axis=0, tiled=True)  16 us
    dot_general x32, matrix products, update(): jnp.einsum('qngd,knd->ngqk', queries, key_matrix, preferred_element_type=...  15.3 us
    all_gather x3, blocking collectives, carried_in(): lax.all_gather(part.astype(kind), axis)  12.7 us
    all_to_all x1, waiting for transfers between devices, softmax_part(): lax.all_to_all(result, 'head', split_axis=0, concat_axis=1, tiled=True)  10.7 us
  transfers between devices with their start and end apart: 5, of which 3 were waited for; matrix products, arithmetic and copies ran while one was open for 42% of the time, Pallas kernels for 0%

commit v1 on v0

--- a/solution.py
+++ b/solution.py
@@ -145,7 +145,9 @@
         result = acc / total[..., None]
         return result.transpose(2, 0, 1, 3).reshape(half, kvl * group * dim).astype(jnp.bfloat16)
 
-    piece = lax.all_gather(local_kv, CTX, axis=0, tiled=True)
+    piece = jnp.concatenate(
+        lax.all_to_all(jnp.stack([local_kv] * lax.axis_size(CTX)), CTX, 0, 0), axis=0
+    )
     rows = piece.shape[0]
     width = math.gcd(rows, 512)
 

time: 222 us -> 244 us (1.099)
  the two profiles are of different devices: /device:TPU:31 before, /device:TPU:30 now
where the time goes in v1:
time: 244 us; the launch traced here: 243 us
  blocking collectives  60.1 us (25%)
  matrix products  48.3 us (20%)
  local copies, waits for them, and re-layouts  35.6 us (15%)
  waiting for transfers between devices  30.7 us (13%)
  other arithmetic  26.1 us (11%)
  starting transfers between devices  23 us (9%)
  between operations  15 us (6%)
  loops' own time  3.77 us (2%)
    all_gather x3, blocking collectives, carried_in(): lax.all_gather(part.astype(kind), axis)  57.6 us
    dot_general x32, matrix products, update(): jnp.einsum('ngqk,knd->ngqd', weights.astype(jnp.bfloat16), value_rows, pr...  26.7 us
    dynamic_slice x32, local copies, waits for them, and re-layouts, step(): kblock = lax.dynamic_slice_in_dim(piece, index * width, width, 0)  17.8 us
    reduce_sum x32, other arithmetic, update(): total = total * decay_factor + jnp.sum(weights, axis=-1)  16.4 us
    all_to_all x1, waiting for transfers between devices, softmax_part(): lax.all_to_all(soft_q, 'head', split_axis=1, concat_axis=0, tiled=True)  16 us
    dot_general x32, matrix products, update(): jnp.einsum('qngd,knd->ngqk', queries, key_matrix, preferred_element_type=...  15.3 us
    all_to_all x1, starting transfers between devices, softmax_part(): lax.all_to_all(soft_kv, 'head', split_axis=1, concat_axis=0, tiled=True)  8.47 us
    all_to_all x1, starting transfers between devices, softmax_part(): lax.all_to_all(jnp.stack([local_kv] * lax.axis_size(CTX)), CTX, 0, 0)  7.5 us
  transfers between devices with their start and end apart: 6, of which 3 were waited for; matrix products, arithmetic and copies ran while one was open for 43% of the time, Pallas kernels for 0%

profile of v1, /device:TPU:30, one launch (start us, length us, event | category | flops | bytes accessed | tf_op | source)
XLA Modules:
  0.0 242.6 jit_solution(10323055746601569506)
XLA Ops:
  8.8 8.5 %all-to-all-start = ((bf16[32,8,256]{2,0,1:T(8,128)(2,1)}), bf16[32,8,256]{2,0,1:T(8,128)(2,1)S(1)}, u32[]{:S(2)}, u32[]{:S(2)}) async-start(bf16[32,8,256]{2,0,1:T(8,128)(2,1)} %bitcast.332), calls=%async_computation | async-start | bytes 262144 | tf_op jit(solution)/shard_map/all_to_all | solution.py:89
  19.1 7.2 %all-to-all-done = bf16[32,8,256]{2,0,1:T(8,128)(2,1)S(1)} async-done(((bf16[32,8,256]{2,0,1:T(8,128)(2,1)}), bf16[32,8,256]{2,0,1:T(8,128)(2,1)S(1)}, u32[]{:S(2)}, u32[]{:S(2)}) %all-to-all-start) | async-done | bytes 131104 | tf_op jit(solution)/shard_map/all_to_all | solution.py:89
  26.4 3.5 %all-to-all-start.2 = ((bf16[32,8,1024]{2,0,1:T(8,128)(2,1)}), bf16[32,8,1024]{2,0,1:T(8,128)(2,1)S(1)}, u32[]{:S(2)}, u32[]{:S(2)}) async-start(bf16[32,8,1024]{2,0,1:T(8,128)(2,1)} %bitcast.331), calls=%async_computation.2 | async-start | bytes 1048576 | tf_op jit(solution)/shard_map/all_to_all | solution.py:88
  30.0 16.0 %all-to-all-done.2 = bf16[32,8,1024]{2,0,1:T(8,128)(2,1)S(1)} async-done(((bf16[32,8,1024]{2,0,1:T(8,128)(2,1)}), bf16[32,8,1024]{2,0,1:T(8,128)(2,1)S(1)}, u32[]{:S(2)}, u32[]{:S(2)}) %all-to-all-start.2) | async-done | bytes 524320 | tf_op jit(solution)/shard_map/all_to_all | solution.py:88
  45.9 2.4 stack.5
  48.4 7.5 %all-to-all-start.1 = ((bf16[32,256,256]{1,2,0:T(8,128)(2,1)}), bf16[32,256,256]{1,2,0:T(8,128)(2,1)}, u32[]{:S(2)}, u32[]{:S(2)}) async-start(bf16[32,256,256]{1,2,0:T(8,128)(2,1)} %stack.5), calls=%async_computation.1 | async-start | bytes 8388608 | tf_op jit(solution)/shard_map/all_to_all | solution.py:149
  58.5 2.4 %all-reduce = bf16[16]{0:T(256)(128)(2,1)S(1)} all-reduce(bf16[16]{0:T(256)(128)(2,1)S(1)} %dynamic-update-slice), channel_id=2, replica_groups=mesh['ctx_0'=4,'ctx_1'=4,'ctx_2'=2,'head'=8] {'ctx_2'}, use_global_device_ids=true, to_apply=%add | all-reduce | flops 16 | bytes 64
  61.7 2.2 all-gather.1
  65.0 48.7 %all-gather.2 = bf16[4,1,8]{2,1,0:T(2,128)(2,1)S(1)} all-gather(bf16[1,1,8]{2,1,0:T(2,128)(2,1)S(1)} %get-tuple-element.626), channel_id=1, replica_groups=mesh['ctx_0'=4,'ctx_1'=4,'ctx_2'=2,'head'=8] {'ctx_1'}, dimensions={0}, use_global_device_ids=true | all-gather | bytes 80 | tf_op jit(solution)/shard_map/all_gather | solution.py:24
  113.8 6.7 %all-gather.3 = bf16[4,1,8]{2,1,0:T(2,128)(2,1)S(1)} all-gather(bf16[1,1,8]{2,1,0:T(2,128)(2,1)S(1)} %get-tuple-element.620), channel_id=1, replica_groups=mesh['ctx_0'=4,'ctx_1'=4,'ctx_2'=2,'head'=8] {'ctx_0'}, dimensions={0}, use_global_device_ids=true | all-gather | bytes 80 | tf_op jit(solution)/shard_map/all_gather | solution.py:24
  120.8 2.3 fusion.66
  123.2 6.4 %copy.101 = bf16[32,256,256]{2,1,0:T(8,128)(2,1)} copy(bf16[32,256,256]{1,2,0:T(8,128)(2,1)} %all-to-all-done.1) | data formatting | bytes 8388608 | tf_op jit(solution)/shard_map/all_to_all | solution.py:149
  129.7 85.3 %while.27 = (s32[]{:T(128)}, f32[1,8,128]{2,1,0:T(8,128)S(1)}, f32[1,8,128]{2,1,0:T(8,128)S(1)}, f32[1,8,128,128]{3,2,1,0:T(8,128)S(1)}, f32[1,8,128]{2,1,0:T(8,...) while((s32[]{:T(128)}, f32[1,8,128]{2,1,0:T(8,128)S(1)}, ...), condition=%wide.region_12.13_spmd.clone, body=%wide.region_3.12_spmd.clone.sunk | while | flops 551165184 | bytes 17445364 | solution.py:161
  130.9 2.1 conditional.7
  133.0 2.1 conditional.6
  136.2 2.1 conditional.7
  138.3 2.1 conditional.6
  141.5 2.1 conditional.7
  143.6 2.1 conditional.6
  146.9 2.1 conditional.7
  148.9 2.1 conditional.6
  152.2 2.1 conditional.7
  154.3 2.1 conditional.6
  157.5 2.1 conditional.7
  159.6 2.1 conditional.6
  162.8 2.1 conditional.7
  164.9 2.1 conditional.6
  168.2 2.1 conditional.7
  170.3 2.1 conditional.6
  173.5 2.1 conditional.7
  175.6 2.1 conditional.6
  178.8 2.1 conditional.7
  180.9 2.1 conditional.6
  184.2 2.1 conditional.7
  186.3 2.1 conditional.6
  189.5 2.1 conditional.7
  191.6 2.1 conditional.6
  194.8 2.1 conditional.7
  196.9 2.1 conditional.6
  200.2 2.1 conditional.7
  205.5 2.1 conditional.7
  207.6 2.1 conditional.6
  210.8 2.1 conditional.7
  212.9 2.1 conditional.6
  216.6 3.5 %all-to-all-start.3 = ((bf16[8,32,1024]{2,1,0:T(8,128)(2,1)}), bf16[8,32,1024]{2,1,0:T(8,128)(2,1)S(1)}, u32[]{:S(2)}, u32[]{:S(2)}) async-start(bf16[8,32,1024]{2,1,0:T(8,128)(2,1)} %bitcast.74), calls=%async_computation.3 | async-start | bytes 1048576 | tf_op jit(solution)/shard_map/all_to_all | solution.py:165
  220.2 3.6 %fusion.41 = f32[256,8,128]{0,2,1:T(8,128)} fusion(f32[256,8]{0,1:T(8,128)S(1)} %get-tuple-element.608, bf16[4,8,128,128]{3,2,1,0:T(8,128)(2,1)} %all-gather.9.cloned.1.call-done, f32[8]{0:T(128)S(1)} %get-tuple-element.627, f32[8]{0:T(128)S(1)} %get-tuple-element.625, f32[8]{0:T(128)S(1)} %get-tuple-element.624, f32[8]{0:T(128)S(1)} %get-tuple-element.623, ...), kind=kOutput, calls=%fused_computation.62 | convolution fusion | flops 72876032 | bytes 4202890 | tf_op jit(solution)/shard_map/thd,hde->the/dot_general | solution.py:56
  223.8 2.4 multiply_reduce_fusion
  227.4 7.5 %all-to-all-done.3 = bf16[8,32,1024]{2,1,0:T(8,128)(2,1)S(1)} async-done(((bf16[8,32,1024]{2,1,0:T(8,128)(2,1)}), bf16[8,32,1024]{2,1,0:T(8,128)(2,1)S(1)}, u32[]{:S(2)}, u32[]{:S(2)}) %all-to-all-start.3) | async-done | bytes 524320 | tf_op jit(solution)/shard_map/all_to_all | solution.py:165
  (421 shorter events, 95.0 us)
Async XLA Ops:
  7.2 213.0 %copy-start = (bf16[256,1024]{1,0:T(8,128)(2,1)S(1)}, bf16[256,1024]{1,0:T(8,128)(2,1)}, u32[]{:S(2)}) copy-start(bf16[256,1024]{1,0:T(8,128)(2,1)} %param.13) | copy-start | bytes 1572868
  8.8 17.6 %all-to-all-start = ((bf16[32,8,256]{2,0,1:T(8,128)(2,1)}), bf16[32,8,256]{2,0,1:T(8,128)(2,1)S(1)}, u32[]{:S(2)}, u32[]{:S(2)}) async-start(bf16[32,8,256]{2,0,1:T(8,128)(2,1)} %bitcast.332), calls=%async_computation | async-start | bytes 262144 | tf_op jit(solution)/shard_map/all_to_all | solution.py:89
  26.4 19.6 %all-to-all-start.2 = ((bf16[32,8,1024]{2,0,1:T(8,128)(2,1)}), bf16[32,8,1024]{2,0,1:T(8,128)(2,1)S(1)}, u32[]{:S(2)}, u32[]{:S(2)}) async-start(bf16[32,8,1024]{2,0,1:T(8,128)(2,1)} %bitcast.331), calls=%async_computation.2 | async-start | bytes 1048576 | tf_op jit(solution)/shard_map/all_to_all | solution.py:88
  48.3 7.6 %copy-start.4 = (f32[8,256]{1,0:T(8,128)S(1)}, f32[8,256]{1,0:T(8,128)}, u32[]{:S(2)}) copy-start(f32[8,256]{1,0:T(8,128)} %param.16) | copy-start | bytes 24580
  48.4 8.4 %copy-start.7 = (u32[256]{0:T(256)S(1)}, u32[256]{0:T(256)}, u32[]{:S(2)}) copy-start(u32[256]{0:T(256)} %constant.123) | copy-start | bytes 3076
  48.4 12.6 %copy-start.1 = (bf16[256,1024]{1,0:T(8,128)(2,1)S(1)}, bf16[256,1024]{1,0:T(8,128)(2,1)}, u32[]{:S(2)}) copy-start(bf16[256,1024]{1,0:T(8,128)(2,1)} %param.14) | copy-start | bytes 1572868
  48.4 13.1 %copy-start.6 = (bf16[256,1024]{1,0:T(8,128)(2,1)S(1)}, bf16[256,1024]{1,0:T(8,128)(2,1)}, u32[]{:S(2)}) copy-start(bf16[256,1024]{1,0:T(8,128)(2,1)} %param.15) | copy-start | bytes 1572868
  48.4 74.8 %all-to-all-start.1 = ((bf16[32,256,256]{1,2,0:T(8,128)(2,1)}), bf16[32,256,256]{1,2,0:T(8,128)(2,1)}, u32[]{:S(2)}, u32[]{:S(2)}) async-start(bf16[32,256,256]{1,2,0:T(8,128)(2,1)} %stack.5), calls=%async_computation.1 | async-start | bytes 8388608 | tf_op jit(solution)/shard_map/all_to_all | solution.py:149
  55.9 64.9 %all-gather.7.cloned.1.call-start = ((), (), s32[]{:S(2)}) async-start(), calls=%async_computation.4 | async-start | bytes 1310720 | tf_op jit(solution)/shard_map/all_gather | solution.py:24
  61.1 59.5 %copy-start.2 = (bf16[256,1024]{0,1:T(8,128)(2,1)}, bf16[256,1024]{0,1:T(8,128)(2,1)S(1)}, u32[]{:S(2)}) copy-start(bf16[256,1024]{0,1:T(8,128)(2,1)S(1)} %copy.119) | copy-start | bytes 1572868
  64.9 155.2 %all-gather.9.cloned.1.call-start = ((), (), s32[]{:S(2)}) async-start(), calls=%async_computation.5 | async-start | bytes 1310720 | tf_op jit(solution)/shard_map/all_gather | solution.py:24
  216.6 18.3 %all-to-all-start.3 = ((bf16[8,32,1024]{2,1,0:T(8,128)(2,1)}), bf16[8,32,1024]{2,1,0:T(8,128)(2,1)S(1)}, u32[]{:S(2)}, u32[]{:S(2)}) async-start(bf16[8,32,1024]{2,1,0:T(8,128)(2,1)} %bitcast.74), calls=%async_computation.3 | async-start | bytes 1048576 | tf_op jit(solution)/shard_map/all_to_all | solution.py:165
  220.2 3.6 %copy-start.3 = (bf16[256,1024]{0,1:T(8,128)(2,1)S(1)}, bf16[256,1024]{0,1:T(8,128)(2,1)}, u32[]{:S(2)}) copy-start(bf16[256,1024]{0,1:T(8,128)(2,1)} %copy-done.2) | copy-start | bytes 1572868
  223.8 2.4 %copy-start.5 = (f32[1024]{0:T(1024)S(1)}, f32[1024]{0:T(1024)}, u32[]{:S(2)}) copy-start(f32[1024]{0:T(1024)} %param.17) | copy-start | bytes 12292
Sparse Core Ops, SparseCore 0:
  65.0 48.0 all-gather.6
  123.3 22.1 all-gather.8
